TPU v7x, 32 devices: a whole 2x2x4 slice. The times are simulated.
32 devices in a mesh: dp: 2 (over x), fsdp: 16 (over z, y, core).
Axes of the slice: x: 2, y: 2, z: 4, core: 2. Of those that a mesh axis runs over, the one named last changes fastest.
Arguments:
- tokens: bfloat16 [16384, 768], P(('dp', 'fsdp')), may hold values from -6 to 6
- cotangent: bfloat16 [16384, 768], P(('dp', 'fsdp')), may hold values from -6 to 6
- image_ids: int32 [16384], P(('dp', 'fsdp')), may hold values from 0 to 2, as said below
- in_weight: float32 [768, 5376], P('fsdp'), may hold values from -0.21875 to 0.21875
- out_weight: float32 [3840, 768], P('fsdp'), may hold values from -1.5 to 1.5
- vectors: float32 [4, 768], P(None, 'fsdp'), may hold values from -1.5 to 1.5
- in_moment: float32 [768, 5376], P('fsdp'), may hold values from -0.66 to 0.66
- out_moment: float32 [3840, 768], P('fsdp'), may hold values from -0.66 to 0.66
- vec_moment: float32 [4, 768], P(None, 'fsdp'), may hold values from -0.66 to 0.66
- in_second: float32 [768, 5376], P('fsdp'), may hold values from 0.01 to 0.1
- out_second: float32 [3840, 768], P('fsdp'), may hold values from 0.01 to 0.1
- vec_second: float32 [4, 768], P(None, 'fsdp'), may hold values from 0.01 to 0.1
Outputs:
- activations: bfloat16 [16384, 768], P(('dp', 'fsdp'))
- input_grad: float32 [16384, 768], P(('dp', 'fsdp'))
- in_grad: float32 [768, 5376], P('fsdp')
- out_grad: float32 [3840, 768], P('fsdp')
- vec_grad: float32 [4, 768], P(None, 'fsdp')
- grad_norm: float32 [], replicated
- in_update: float32 [768, 5376], P('fsdp')
- out_update: float32 [3840, 768], P('fsdp')
- vec_update: float32 [4, 768], P(None, 'fsdp')
- in_mean: float32 [768, 5376], P('fsdp')
- out_mean: float32 [3840, 768], P('fsdp')
- vec_mean: float32 [4, 768], P(None, 'fsdp')
- in_square: float32 [768, 5376], P('fsdp')
- out_square: float32 [3840, 768], P('fsdp')
- vec_square: float32 [4, 768], P(None, 'fsdp')
Inputs may be any that keep to these rules, and one draw needn't show every extreme that they name: `image_ids`: tokens of one image all lie within one device's 512 rows, and ids never decrease along a device's rows. One eighth of the devices each hold a single image of 512 tokens with id 0; every other device holds images of 196 tokens numbered 0, 1, 2, ... followed by one shorter image.
All inputs are finite; a program needn't handle non-finite values.
Results may differ from a plain program's by a relative error of at most 0.02.
Values may be sent and summed in bfloat16 or wider, within the bound.
No kernel may reach another device: no remote copies, remote signals or barrier semaphores. Data moves between devices by JAX's collectives and lax.ppermute only.
A program may use at most 128 MiB of HBM per device.

v0:
```python
import math
import jax
import jax.numpy as jnp
from jax import lax
from jax.sharding import PartitionSpec as P

D = 768
H = 12
HD = 64
ADAM_STEP = 10
PARAMS = 7080960
beta_one = 0.9
beta_two = 0.95
learning = 0.03
decay_rate = 0.1
epsilon = 1e-08
norm_eps = 1e-06
masked = -1e30


def row_norm(values):
    centre = values - jnp.mean(values, axis=-1, keepdims=True)
    spread = jnp.mean(centre * centre, axis=-1, keepdims=True)
    return centre * lax.rsqrt(spread + norm_eps)


def input_norm(rows, gain):
    return row_norm(rows) * gain


def head_norm(raw, gain, factor):
    heads = raw.reshape(raw.shape[0], H, HD)
    return row_norm(heads) * gain.reshape(H, HD) * factor


def activation(values):
    return jax.nn.gelu(values, approximate=True)


def attention_forward(query_lo, key_lo, value_lo, image_ids):
    count = query_lo.shape[0]
    block = min(512, count)
    blocks = count // block

    def one_block(pair):
        query_block, ids_block = pair
        scores = jnp.einsum("qhd,khd->hqk", query_block, key_lo, preferred_element_type=jnp.float32)
        same = (ids_block[:, None] == image_ids[None, :])[None]
        scores = jnp.where(same, scores, masked)
        largest = jnp.max(scores, axis=-1, keepdims=True)
        raised = jnp.exp(scores - largest)
        totals = jnp.sum(raised, axis=-1, keepdims=True)
        probs_lo = (raised / totals).astype(jnp.bfloat16)
        attended = jnp.einsum(
            "hqk,khd->qhd", probs_lo, value_lo, preferred_element_type=jnp.float32
        )
        return (attended, (largest + jnp.log(totals))[:, :, 0])

    attended, log_total = lax.map(
        one_block, (query_lo.reshape(blocks, block, H, HD), image_ids.reshape(blocks, block))
    )
    return (attended.reshape(count, H, HD), log_total)


def attention_backward(query_lo, key_lo, value_lo, image_ids, log_total, d_attended):
    count = query_lo.shape[0]
    block = min(512, count)
    blocks = count // block

    def one_block(carry, pieces):
        key_acc, value_acc = carry
        query_block, ids_block, total_block, grad_block = pieces
        scores = jnp.einsum("qhd,khd->hqk", query_block, key_lo, preferred_element_type=jnp.float32)
        same = (ids_block[:, None] == image_ids[None, :])[None]
        scores = jnp.where(same, scores, masked)
        probs = jnp.exp(scores - total_block[:, :, None])
        probs_lo = probs.astype(jnp.bfloat16)
        value_acc = value_acc + jnp.einsum(
            "hqk,qhd->khd", probs_lo, grad_block, preferred_element_type=jnp.float32
        )
        d_probs = jnp.einsum(
            "qhd,khd->hqk", grad_block, value_lo, preferred_element_type=jnp.float32
        )
        centre = jnp.sum(probs * d_probs, axis=-1, keepdims=True)
        d_scores = (probs * (d_probs - centre)).astype(jnp.bfloat16)
        d_query = jnp.einsum("hqk,khd->qhd", d_scores, key_lo, preferred_element_type=jnp.float32)
        key_acc = key_acc + jnp.einsum(
            "hqk,qhd->khd", d_scores, query_block, preferred_element_type=jnp.float32
        )
        return ((key_acc, value_acc), d_query)

    zeros = jnp.zeros((count, H, HD), jnp.float32)
    pieces = (
        query_lo.reshape(blocks, block, H, HD),
        image_ids.reshape(blocks, block),
        log_total,
        d_attended.reshape(blocks, block, H, HD),
    )
    (d_key, d_value), d_query = lax.scan(one_block, (zeros, zeros), pieces)
    return (d_query.reshape(count, H, HD), d_key, d_value)


def forward_pass(tokens, image_ids, full):
    full_in, full_out, full_vec = full
    gains = full_vec.astype(jnp.float32)
    rows = tokens.astype(jnp.float32)
    scaled_lo = input_norm(rows, gains[0]).astype(jnp.bfloat16)
    hidden = jnp.dot(scaled_lo, full_in, preferred_element_type=jnp.float32)
    query_raw = hidden[:, :D]
    key_raw = hidden[:, D : 2 * D]
    value_lo = hidden[:, 2 * D : 3 * D].astype(jnp.bfloat16).reshape(-1, H, HD)
    inner = hidden[:, 3 * D :]
    query_lo = head_norm(query_raw, gains[1], HD ** (-0.5)).astype(jnp.bfloat16)
    key_lo = head_norm(key_raw, gains[2], 1.0).astype(jnp.bfloat16)
    attended, log_total = attention_forward(query_lo, key_lo, value_lo, image_ids)
    mixed_lo = jnp.concatenate([attended.reshape(-1, D), activation(inner)], axis=1).astype(
        jnp.bfloat16
    )
    branch = jnp.dot(mixed_lo, full_out, preferred_element_type=jnp.float32) + gains[3]
    result = (rows + branch).astype(jnp.bfloat16)
    return (
        result,
        (scaled_lo, query_raw, key_raw, query_lo, key_lo, value_lo, inner, mixed_lo, log_total),
    )


def backward_pass(tokens, cotangent, image_ids, full, saved):
    full_in, full_out, full_vec = full
    gains = full_vec.astype(jnp.float32)
    scaled_lo, query_raw, key_raw, query_lo, key_lo, value_lo, inner, mixed_lo, log_total = saved
    contract_rows = (((0,), (0,)), ((), ()))
    contract_cols = (((1,), (1,)), ((), ()))
    out_grad = lax.dot_general(
        mixed_lo, cotangent, contract_rows, preferred_element_type=jnp.float32
    )
    d_mixed = lax.dot_general(
        cotangent, full_out, contract_cols, preferred_element_type=jnp.float32
    ).astype(jnp.bfloat16)
    d_attended = d_mixed[:, :D].reshape(-1, H, HD)
    d_query, d_key, d_value = attention_backward(
        query_lo, key_lo, value_lo, image_ids, log_total, d_attended
    )
    d_inner = jax.vjp(activation, inner)[1](d_mixed[:, D:].astype(jnp.float32))[0]
    query_back = jax.vjp(lambda raw, gain: head_norm(raw, gain, HD ** (-0.5)), query_raw, gains[1])[
        1
    ]
    key_back = jax.vjp(lambda raw, gain: head_norm(raw, gain, 1.0), key_raw, gains[2])[1]
    d_query_raw, d_query_gain = query_back(d_query)
    d_key_raw, d_key_gain = key_back(d_key)
    d_hidden = jnp.concatenate(
        [d_query_raw, d_key_raw, d_value.reshape(-1, D), d_inner], axis=1
    ).astype(jnp.bfloat16)
    in_grad = lax.dot_general(
        scaled_lo, d_hidden, contract_rows, preferred_element_type=jnp.float32
    )
    d_scaled = lax.dot_general(d_hidden, full_in, contract_cols, preferred_element_type=jnp.float32)
    rows = tokens.astype(jnp.float32)
    norm_back = jax.vjp(input_norm, rows, gains[0])[1]
    d_rows, d_norm_gain = norm_back(d_scaled)
    cot_rows = cotangent.astype(jnp.float32)
    input_grad = cot_rows + d_rows
    vec_grad = jnp.stack([d_norm_gain, d_query_gain, d_key_gain, jnp.sum(cot_rows, axis=0)], axis=0)
    return (input_grad, in_grad, out_grad, vec_grad)


def square_total(partial_sum):
    return lax.psum(partial_sum, "fsdp")


def adamw(master, first, second, grad, factor):
    clipped = grad * factor
    first_new = beta_one * first + (1.0 - beta_one) * clipped
    second_new = beta_two * second + (1.0 - beta_two) * clipped * clipped
    first_hat = first_new / (1.0 - beta_one**ADAM_STEP)
    second_hat = second_new / (1.0 - beta_two**ADAM_STEP)
    update = -learning * (first_hat / (jnp.sqrt(second_hat) + epsilon) + decay_rate * master)
    return (update, first_new, second_new)


def local(
    tokens,
    cotangent,
    image_ids,
    in_weight,
    out_weight,
    vectors,
    in_moment,
    out_moment,
    vec_moment,
    in_second,
    out_second,
    vec_second,
):
    low_in = in_weight.astype(jnp.bfloat16)
    low_out = out_weight.astype(jnp.bfloat16)
    low_vec = vectors.astype(jnp.bfloat16)
    full = (
        lax.all_gather(low_in, "fsdp", axis=0, tiled=True),
        lax.all_gather(low_out, "fsdp", axis=0, tiled=True),
        lax.all_gather(low_vec, "fsdp", axis=1, tiled=True),
    )
    result, saved = forward_pass(tokens, image_ids, full)
    full = (
        lax.all_gather(low_in, "fsdp", axis=0, tiled=True),
        lax.all_gather(low_out, "fsdp", axis=0, tiled=True),
        lax.all_gather(low_vec, "fsdp", axis=1, tiled=True),
    )
    unused, saved = forward_pass(tokens, image_ids, full)
    input_grad, in_local, out_local, vec_local = backward_pass(
        tokens, cotangent, image_ids, full, saved
    )
    in_part, out_part, vec_part = (
        lax.psum_scatter(
            in_local.astype(jnp.bfloat16), "fsdp", scatter_dimension=0, tiled=True
        ).astype(jnp.float32),
        lax.psum_scatter(
            out_local.astype(jnp.bfloat16), "fsdp", scatter_dimension=0, tiled=True
        ).astype(jnp.float32),
        lax.psum_scatter(
            vec_local.astype(jnp.bfloat16), "fsdp", scatter_dimension=1, tiled=True
        ).astype(jnp.float32),
    )
    in_grad, out_grad, vec_grad = lax.psum((in_part, out_part, vec_part), "dp")
    total = square_total(
        jnp.sum(in_grad * in_grad) + jnp.sum(out_grad * out_grad) + jnp.sum(vec_grad * vec_grad)
    )
    grad_norm = jnp.sqrt(total)
    factor = jnp.minimum(1.0, math.sqrt(PARAMS) / grad_norm)
    in_update, in_mean, in_square = adamw(in_weight, in_moment, in_second, in_grad, factor)
    out_update, out_mean, out_square = adamw(out_weight, out_moment, out_second, out_grad, factor)
    vec_update, vec_mean, vec_square = adamw(vectors, vec_moment, vec_second, vec_grad, factor)
    return (
        result,
        input_grad,
        in_grad,
        out_grad,
        vec_grad,
        grad_norm,
        in_update,
        out_update,
        vec_update,
        in_mean,
        out_mean,
        vec_mean,
        in_square,
        out_square,
        vec_square,
    )


def solution(mesh):
    in_specs = (
        P(("dp", "fsdp"), None),
        P(("dp", "fsdp"), None),
        P(("dp", "fsdp")),
        P("fsdp", None),
        P("fsdp", None),
        P(None, "fsdp"),
        P("fsdp", None),
        P("fsdp", None),
        P(None, "fsdp"),
        P("fsdp", None),
        P("fsdp", None),
        P(None, "fsdp"),
    )
    out_specs = (
        P(("dp", "fsdp"), None),
        P(("dp", "fsdp"), None),
        P("fsdp", None),
        P("fsdp", None),
        P(None, "fsdp"),
        P(),
        P("fsdp", None),
        P("fsdp", None),
        P(None, "fsdp"),
        P("fsdp", None),
        P("fsdp", None),
        P(None, "fsdp"),
        P("fsdp", None),
        P("fsdp", None),
        P(None, "fsdp"),
    )
    return jax.shard_map(local, mesh=mesh, in_specs=in_specs, out_specs=out_specs, check_vma=False)
```

profile of v0, /device:TPU:0, one launch (start us, length us, event | category | flops | bytes accessed | tf_op | source)
XLA Modules:
  0.0 581.6 jit_solution(2606356663764410176)
XLA Ops:
  7.2 2.0 convert_element_type.86
  11.0 23.1 %all-gather = bf16[16,48,4]{1,2,0:T(4,128)(2,1)S(1)} all-gather(bf16[1,48,4]{1,2,0:T(4,128)(2,1)S(1)} %convert_bitcast_fusion), channel_id=1, replica_groups=mesh['dp'=2,'fsdp'=16] {'fsdp'}, dimensions={0}, use_global_device_ids=true | all-gather | bytes 6528 | tf_op jit(solution)/shard_map/all_gather | solution.py:200
  35.8 37.3 %all-gather.6.cloned.1.call-done = bf16[3840,768]{1,0:T(8,128)(2,1)} async-done(((bf16[240,768]{1,0:T(8,128)(2,1)}), bf16[3840,768]{1,0:T(8,128)(2,1)}) %all-gather.6.cloned.1.call-update) | async-done | bytes 5898256 | tf_op jit(solution)/shard_map/all_gather | solution.py:199
  73.1 6.2 %convolution_convert_fusion.2 = bf16[512,3840]{1,0:T(8,128)(2,1)S(1)} fusion(bf16[512,768]{1,0:T(8,128)(2,1)S(1)} %copy-done.12, bf16[3840,768]{1,0:T(8,128)(2,1)} %all-gather.6.cloned.1.call-done), kind=kOutput, calls=%fused_computation.30 | convolution fusion | flops 3021864960 | bytes 10616832 | tf_op jit(solution)/shard_map/dot_general | solution.py:136
  82.4 66.3 %all-gather.4.cloned.1.call-done = bf16[768,5376]{1,0:T(8,128)(2,1)} async-done(((bf16[48,5376]{1,0:T(8,128)(2,1)}), bf16[768,5376]{1,0:T(8,128)(2,1)}) %all-gather.4.cloned.1.call-update) | async-done | bytes 8257552 | tf_op jit(solution)/shard_map/all_gather | solution.py:198
  148.7 7.2 %fusion.56 = f32[512,5376]{1,0:T(8,128)S(1)} fusion(bf16[768,5376]{1,0:T(8,128)(2,1)} %all-gather.4.cloned.1.call-done, bf16[512,768]{1,0:T(8,128)(2,1)S(1)} %copy-done.3, f32[768]{0:T(1024)S(1)} %get-tuple-element.91, f32[512]{0:T(512)S(1)} %fusion.47, f32[512]{0:T(512)S(1)} %broadcast_multiply_fusion.3), kind=kOutput, calls=%fused_computation.122 | convolution fusion | flops 4229824512 | bytes 20061184 | tf_op jit(solution)/shard_map/dot_general | solution.py:108
  156.0 7.0 %fusion.4 = (bf16[512,3072]{1,0:T(8,128)(2,1)}, bf16[512,3072]{1,0:T(8,128)(2,1)}) fusion(f32[512,5376]{1,0:T(8,128)S(1)} %fusion.56, bf16[512,3840]{1,0:T(8,128)(2,1)S(1)} %copy-done.9), kind=kLoop, calls=%fused_computation.16 | loop fusion | flops 36175872 | bytes 15728640 | tf_op jit(solution)/shard_map/convert.11
  170.5 2.5 select_reduce_fusion
  173.0 2.2 fusion
  175.3 5.8 fusion.36
  181.1 3.6 fusion.33
  184.6 7.2 %multiply_reduce_fusion = (f32[12,512]{1,0:T(8,128)}, f32[12,512,512]{1,2,0:T(8,128)}) fusion(f32[12,512,512]{1,2,0:T(8,128)S(1)} %get-tuple-element.120, f32[12,512]{1,0:T(8,128)S(1)} %log_add_fusion, pred[512,512]{0,1:T(8,128)(4,1)S(1)} %broadcast_compare_fusion, bf16[512,12,64]{0,2,1:T(8,128)(2,1)S(1)} %bitcast.76, bf16[512,12,64]{0,2,1:T(8,128)(2,1)S(1)} %bitcast.78), kind=kOutput, calls=%fused_computation.1 | convolution fusion | flops 415229952 | bytes 27049984 | tf_op jit(solution)/shard_map/while/body/eval_jaxpr/qhd,khd->hqk/dot_general | solution.py:81
  191.8 2.3 copy.72
  194.1 2.3 copy.79
  196.4 9.9 %multiply_convert_fusion = bf16[12,512,512]{1,2,0:T(8,128)(2,1)S(1)} fusion(f32[12,512,512]{1,2,0:T(8,128)} %get-tuple-element.122, f32[12,512,512]{1,2,0:T(8,128)} %copy-done, f32[12,512]{1,0:T(8,128)} %get-tuple-element.121, f32[12,512]{1,0:T(8,128)} %copy-done.24, pred[512,512]{0,1:T(8,128)(4,1)S(1)} %broadcast_compare_fusion), kind=kLoop, calls=%fused_computation | loop fusion | flops 15728640 | bytes 31768576 | tf_op jit(solution)/shard_map/while/body/eval_jaxpr/convert_element_type | solution.py:85
  206.3 2.1 multiply_reduce_fusion.1
  208.5 2.5 fusion.32
  213.3 2.9 add_convert_fusion
  216.2 2.4 copy.78
  222.0 2.4 copy.77
  224.4 9.0 %fusion.28 = (f32[512]{0:T(512)S(1)}, f32[512,768]{1,0:T(8,128)S(1)}) fusion(bf16[512,768]{1,0:T(8,128)(2,1)S(1)} %copy-done.4, f32[768]{0:T(1024)S(1)} %copy-done.29, f32[512]{0:T(512)S(1)} %copy-done.31, bf16[768,5376]{1,0:T(8,128)(2,1)} %all-gather.4.cloned.1.call-done, bf16[512,3072]{1,0:T(8,128)(2,1)} %get-tuple-element.115, ...), kind=kOutput, calls=%fused_computation.49 | convolution fusion | flops 4251844096 | bytes 16129024 | tf_op jit(solution)/shard_map/dot_general | solution.py:156
  235.4 7.9 %convolution_convert_fusion.1 = bf16[3840,768]{1,0:T(8,128)(2,1)} fusion(bf16[512,768]{1,0:T(8,128)(2,1)S(1)} %copy-done.13, bf16[512,3072]{1,0:T(8,128)(2,1)} %get-tuple-element.116, bf16[512,768]{1,0:T(8,128)(2,1)} %copy.72), kind=kOutput, calls=%fused_computation.13 | convolution fusion | flops 3030712320 | bytes 10616832 | tf_op jit(solution)/shard_map/dot_general | solution.py:133
  244.5 10.2 %convolution_convert_fusion = bf16[768,5376]{1,0:T(8,128)(2,1)} fusion(bf16[512,3072]{1,0:T(8,128)(2,1)} %get-tuple-element.115, bf16[512,768]{1,0:T(8,128)(2,1)S(1)} %copy-done.18, bf16[512,768]{1,0:T(8,128)(2,1)} %copy.78, bf16[512,768]{1,0:T(8,128)(2,1)} %copy.77, bf16[512,768]{1,0:T(8,128)(2,1)S(1)} %copy-done.4, f32[768]{0:T(1024)S(1)} %copy-done.29, ...), kind=kOutput, calls=%fused_computation.7 | convolution fusion | flops 4255973376 | bytes 14556160 | tf_op jit(solution)/shard_map/dot_general | solution.py:153
  255.8 7.7 %fusion.29 = bf16[512,768]{1,0:T(8,128)(2,1)} fusion(bf16[512,768]{1,0:T(8,128)(2,1)S(1)} %copy-done.4, bf16[3840,768]{1,0:T(8,128)(2,1)} %all-gather.6.cloned.1.call-done, bf16[512,3072]{1,0:T(8,128)(2,1)} %get-tuple-element.116, bf16[512,768]{1,0:T(8,128)(2,1)S(1)} %copy-done.16, f32[768]{0:T(1024)S(1)} %copy-done.42), kind=kOutput, calls=%fused_computation.50 | convolution fusion | flops 3029336064 | bytes 11406336 | tf_op jit(solution)/shard_map/dot_general | solution.py:119
  263.5 23.7 %reduce-scatter.10.cloned.1.call-done = bf16[48,4]{1,0:T(8,128)(2,1)} async-done(((bf16[768,4]{1,0:T(8,128)(2,1)}), bf16[48,4]{1,0:T(8,128)(2,1)}) %reduce-scatter.10.cloned.1.call-update) | async-done | bytes 400
  288.0 84.8 %reduce-scatter.8.cloned.1.call-done = bf16[240,768]{1,0:T(8,128)(2,1)} async-done(((bf16[3840,768]{1,0:T(8,128)(2,1)}), bf16[240,768]{1,0:T(8,128)(2,1)}) %reduce-scatter.8.cloned.1.call-update) | async-done | bytes 368656 | tf_op jit(solution)/shard_map/reduce_scatter | solution.py:216
  372.7 107.5 %reduce-scatter.6.cloned.1.call-done = bf16[48,5376]{1,0:T(8,128)(2,1)} async-done(((bf16[768,5376]{1,0:T(8,128)(2,1)}), bf16[48,5376]{1,0:T(8,128)(2,1)}) %reduce-scatter.6.cloned.1.call-update) | async-done | bytes 516112 | tf_op jit(solution)/shard_map/reduce_scatter | solution.py:213
  480.2 46.3 %all-reduce.2 = (f32[48,5376]{1,0:T(8,128)S(1)}, f32[240,768]{1,0:T(8,128)}, f32[4,48]{1,0:T(4,128)S(1)}) all-reduce(bf16[48,5376]{1,0:T(8,128)(2,1)} %reduce-scatter.6.cloned.1.call-done, bf16[240,768]{1,0:T(8,128)(2,1)} %reduce-scatter.8.cloned.1.call-done, bf16[4,48]{1,0:T(4,128)(2,1)S(1)} %copy.85), channel_id=1, replica_groups=mesh['dp'=2,'fsdp'=16] {'dp'}, use_global_device_ids=true, to_apply=%region_16.17 | all-reduce | flops 442560 | bytes 2655360 | tf_op jit(solution)/shard_map/psum | solution.py:223
  532.0 2.9 add_add_fusion.3
  534.8 31.6 %psum.31 = f32[]{:T(128)} all-reduce(f32[]{:T(128)S(6)} %add.160), channel_id=1, replica_groups=mesh['dp'=2,'fsdp'=16] {'fsdp'}, use_global_device_ids=true, to_apply=%region_28.29 | all-reduce | flops 1 | bytes 8 | tf_op jit(solution)/shard_map/psum | solution.py:167
  567.9 3.6 add_multiply_fusion.1
  571.5 2.2 add_multiply_fusion
  (150 shorter events, 28.8 us)
Async XLA Ops:
  7.2 3.1 copy-start.12
  7.2 65.9 %all-gather.6.cloned.1.call-start = ((), (), s32[]{:S(2)}) async-start(), calls=%async_computation.4 | async-start | bytes 6266880 | tf_op jit(solution)/shard_map/all_gather | solution.py:199
  9.3 25.7 %copy-start.3 = (bf16[512,768]{1,0:T(8,128)(2,1)S(1)}, bf16[512,768]{1,0:T(8,128)(2,1)}, u32[]{:S(2)}) copy-start(bf16[512,768]{1,0:T(8,128)(2,1)} %param.12) | copy-start | bytes 2359300
  9.3 139.4 %all-gather.4.cloned.1.call-start = ((), (), s32[]{:S(2)}) async-start(), calls=%async_computation.3 | async-start | bytes 8773632 | tf_op jit(solution)/shard_map/all_gather | solution.py:198
  10.2 25.4 %copy-start.38 = (s32[512]{0:T(512)S(1)}, s32[512]{0:T(512)}, u32[]{:S(2)}) copy-start(s32[512]{0:T(512)} %param.14) | copy-start | bytes 6148
  10.2 277.0 %reduce-scatter.10.cloned.1.call-start = ((), (), s32[]{:S(2)}) async-start(), calls=%async_computation.7 | async-start | bytes 208896
  34.8 113.9 %copy-start.28 = (f32[768]{0:T(1024)}, f32[768]{0:T(1024)S(1)}, u32[]{:S(2)}) copy-start(f32[768]{0:T(1024)S(1)} %get-tuple-element.91) | copy-start | bytes 9220
  35.0 44.3 %copy-start.25 = (f32[12,64]{1,0:T(8,128)}, f32[12,64]{1,0:T(8,128)S(1)}, u32[]{:S(2)}) copy-start(f32[12,64]{1,0:T(8,128)S(1)} %mul.423) | copy-start | bytes 9220
  35.2 113.5 %copy-start.30 = (f32[512]{0:T(512)}, f32[512]{0:T(512)S(1)}, u32[]{:S(2)}) copy-start(f32[512]{0:T(512)S(1)} %broadcast_multiply_fusion.3) | copy-start | bytes 6148
  35.5 43.8 %copy-start.32 = (f32[512]{0:T(512)}, f32[512]{0:T(512)S(1)}, u32[]{:S(2)}) copy-start(f32[512]{0:T(512)S(1)} %fusion.27) | copy-start | bytes 6148
  35.6 113.2 %copy-start.34 = (f32[512]{0:T(512)}, f32[512]{0:T(512)S(1)}, u32[]{:S(2)}) copy-start(f32[512]{0:T(512)S(1)} %fusion.47) | copy-start | bytes 6148
  148.7 7.3 %copy-start.9 = (bf16[512,3840]{1,0:T(8,128)(2,1)S(1)}, bf16[512,3840]{1,0:T(8,128)(2,1)}, u32[]{:S(2)}) copy-start(bf16[512,3840]{1,0:T(8,128)(2,1)} %copy-done.8) | copy-start | bytes 11796484
  173.0 11.6 %copy-start = (f32[12,512,512]{1,2,0:T(8,128)}, f32[12,512,512]{1,2,0:T(8,128)S(1)}, u32[]{:S(2)}) copy-start(f32[12,512,512]{1,2,0:T(8,128)S(1)} %get-tuple-element.120) | copy-start | bytes 37748740
  175.3 9.4 %copy-start.24 = (f32[12,512]{1,0:T(8,128)}, f32[12,512]{1,0:T(8,128)S(1)}, u32[]{:S(2)}) copy-start(f32[12,512]{1,0:T(8,128)S(1)} %log_add_fusion) | copy-start | bytes 73732
  175.3 5.8 copy-start.10
  181.1 3.6 copy-start.11
  196.4 9.9 %copy-start.27 = (f32[12,64]{1,0:T(8,128)S(1)}, f32[12,64]{1,0:T(8,128)}, u32[]{:S(2)}) copy-start(f32[12,64]{1,0:T(8,128)} %copy-done.25) | copy-start | bytes 9220
  208.4 3.2 copy-start.2
  208.5 3.2 copy-start.23
  220.5 3.9 copy-start.29
  224.4 9.0 %copy-start.33 = (f32[512]{0:T(512)S(1)}, f32[512]{0:T(512)}, u32[]{:S(2)}) copy-start(f32[512]{0:T(512)} %copy-done.32) | copy-start | bytes 6148
  224.4 9.0 %copy-start.35 = (f32[512]{0:T(512)S(1)}, f32[512]{0:T(512)}, u32[]{:S(2)}) copy-start(f32[512]{0:T(512)} %copy-done.34) | copy-start | bytes 6148
  235.2 137.6 %reduce-scatter.8.cloned.1.call-start = ((), (), s32[]{:S(2)}) async-start(), calls=%async_computation.6 | async-start | bytes 6266880 | tf_op jit(solution)/shard_map/reduce_scatter | solution.py:216
  243.4 236.8 %reduce-scatter.6.cloned.1.call-start = ((), (), s32[]{:S(2)}) async-start(), calls=%async_computation.5 | async-start | bytes 8773632 | tf_op jit(solution)/shard_map/reduce_scatter | solution.py:213
  526.5 40.7 %copy-start.39 = (f32[4,48]{1,0:T(4,128)}, f32[4,48]{1,0:T(4,128)S(1)}, u32[]{:S(2)}) copy-start(f32[4,48]{1,0:T(4,128)S(1)} %get-tuple-element.105) | copy-start | bytes 2308
  526.5 45.0 %copy-start.7 = (f32[48,5376]{1,0:T(8,128)}, f32[48,5376]{1,0:T(8,128)S(1)}, u32[]{:S(2)}) copy-start(f32[48,5376]{1,0:T(8,128)S(1)} %get-tuple-element.92) | copy-start | bytes 3096580
  531.9 35.3 %copy-start.41 = (f32[4,48]{1,0:T(4,128)S(1)}, f32[4,48]{1,0:T(4,128)}, u32[]{:S(2)}) copy-start(f32[4,48]{1,0:T(4,128)} %param.17) | copy-start | bytes 2308
  532.0 35.3 %copy-start.43 = (f32[4,48]{1,0:T(4,128)S(1)}, f32[4,48]{1,0:T(4,128)}, u32[]{:S(2)}) copy-start(f32[4,48]{1,0:T(4,128)} %param.20) | copy-start | bytes 2308
  532.0 35.3 %copy-start.44 = (f32[4,48]{1,0:T(4,128)S(1)}, f32[4,48]{1,0:T(4,128)}, u32[]{:S(2)}) copy-start(f32[4,48]{1,0:T(4,128)} %param.23) | copy-start | bytes 2308
  567.9 3.6 copy-start.6
  567.9 3.6 copy-start.14
  567.9 3.6 copy-start.15
  (18 other events, 29.8 us)
Sparse Core Ops, SparseCore 0:
  10.9 62.2 all-gather.5
  76.0 72.6 all-gather.3
  235.3 51.8 reduce-scatter.9
  291.0 81.7 reduce-scatter.7
  377.2 102.9 reduce-scatter.5
where the time goes:
time: 588 us; the launch traced here: 582 us
  waiting for transfers between devices  320 us (54%)
  blocking collectives  101 us (17%)
  matrix products  71.7 us (12%)
  other arithmetic  45.7 us (8%)
  local copies, waits for them, and re-layouts  24.6 us (4%)
  between operations  18.4 us (3%)
    reduce_scatter x1, waiting for transfers between devices, local(): lax.psum_scatter(in_local.astype(jnp.bfloat16), 'fsdp', scatter_dimension...  107 us
    reduce_scatter x1, waiting for transfers between devices, local(): lax.psum_scatter(out_local.astype(jnp.bfloat16), 'fsdp', scatter_dimensio...  84.8 us
    all_gather x1, waiting for transfers between devices, local(): lax.all_gather(low_in, 'fsdp', axis=0, tiled=True)  66.3 us
    psum x1, blocking collectives, local(): in_grad, out_grad, vec_grad = lax.psum((in_part, out_part, vec_part), 'dp')  46.3 us
    all_gather x1, waiting for transfers between devices, local(): lax.all_gather(low_out, 'fsdp', axis=0, tiled=True)  37.3 us
    psum x1, blocking collectives, square_total(): return lax.psum(partial_sum, 'fsdp')  31.6 us
    unnamed x6, waiting for transfers between devices  23.7 us
    all_gather x1, blocking collectives, local(): lax.all_gather(low_vec, 'fsdp', axis=1, tiled=True)  23.1 us
  transfers between devices with their start and end apart: 5, of which 5 were waited for; matrix products, arithmetic and copies ran while one was open for 6% of the time, Pallas kernels for 0%

commit v1 on v0

--- a/solution.py
+++ b/solution.py
@@ -16,6 +16,19 @@
 epsilon = 1e-08
 norm_eps = 1e-06
 masked = -1e30
+
+
+def gather_around(x, axis, dim):
+    ways = lax.axis_size(axis)
+    up = [(d, (d + 1) % ways) for d in range(ways)]
+    down = [(d, (d - 1) % ways) for d in range(ways)]
+    earlier, later = ([x], [x])
+    for _ in range(ways // 2):
+        earlier.append(lax.ppermute(earlier[-1], axis, up))
+    for _ in range((ways - 1) // 2):
+        later.append(lax.ppermute(later[-1], axis, down))
+    line = jnp.concatenate([*earlier[::-1], *later[1:]], axis=dim)
+    return jnp.roll(line, (lax.axis_index(axis) - ways // 2) * x.shape[dim], axis=dim)
 
 
 def row_norm(values):
@@ -197,7 +210,7 @@
     full = (
         lax.all_gather(low_in, "fsdp", axis=0, tiled=True),
         lax.all_gather(low_out, "fsdp", axis=0, tiled=True),
-        lax.all_gather(low_vec, "fsdp", axis=1, tiled=True),
+        gather_around(low_vec, "fsdp", 1),
     )
     result, saved = forward_pass(tokens, image_ids, full)
     full = (

time: 588 us -> 592 us (level)
  waiting for transfers between devices: 320 us -> 250 us
  starting transfers between devices: 0.42 us -> 31.6 us
  matrix products: 71.7 us -> 91.7 us
  local copies, waits for them, and re-layouts: 24.6 us -> 39.3 us
  other arithmetic: 45.7 us -> 52.4 us
    reduce_scatter x1, waiting for transfers between devices: 84.8 us -> 23.6 us  [local(): lax.psum_scatter(out_local.astype(jnp.bfloat16), 'fsdp', scatter_dimensio...]
    ppermute x0 -> x15, starting transfers between devices: none -> 31 us  [the longest x7 30.6 us: gather_around(): later.append(lax.ppermute(later[-1], axis, down))]
    unnamed x6, waiting for transfers between devices: 23.7 us -> 0.08 us
    ppermute x0 -> x15, waiting for transfers between devices: none -> 14.7 us  [the longest x8 14.4 us: gather_around(): earlier.append(lax.ppermute(earlier[-1], axis, up))]
    sub x0 -> x1, matrix products: none -> 8.88 us  [one_block(): raised = jnp.exp(scores - largest)]
    dot_general x1 -> x2, matrix products: 7.16 us -> 14.6 us  [forward_pass(): hidden = jnp.dot(scaled_lo, full_in, preferred_element_type=jnp.float32)]
    dot_general x1 -> x2, matrix products: 5.77 us -> 11.7 us  [one_block(): jnp.einsum('hqk,khd->qhd', probs_lo, value_lo, preferred_element_type=jnp...]
    another operation x3 -> x4, other arithmetic: 11.3 us -> 15 us
  transfers between devices with their start and end apart: 5 -> 20, of which waited for: 5 -> 17; matrix products, arithmetic and copies ran while one was open for 6% -> 12% of each run, Pallas kernels for 0% -> 0%
where the time goes in v1:
time: 592 us; the launch traced here: 585 us
  waiting for transfers between devices  250 us (42%)
  blocking collectives  101 us (17%)
  matrix products  91.7 us (15%)
  other arithmetic  52.4 us (9%)
  local copies, waits for them, and re-layouts  39.3 us (7%)
  starting transfers between devices  31.6 us (5%)
  between operations  18.6 us (3%)
    reduce_scatter x1, waiting for transfers between devices, local(): lax.psum_scatter(in_local.astype(jnp.bfloat16), 'fsdp', scatter_dimension...  107 us
    all_gather x1, waiting for transfers between devices, local(): lax.all_gather(low_in, 'fsdp', axis=0, tiled=True)  66.3 us
    psum x1, blocking collectives, local(): in_grad, out_grad, vec_grad = lax.psum((in_part, out_part, vec_part), 'dp')  46.3 us
    all_gather x1, waiting for transfers between devices, local(): lax.all_gather(low_out, 'fsdp', axis=0, tiled=True)  38.1 us
    psum x1, blocking collectives, square_total(): return lax.psum(partial_sum, 'fsdp')  31.6 us
    ppermute x7, starting transfers between devices, gather_around(): later.append(lax.ppermute(later[-1], axis, down))  30.6 us
    reduce_scatter x1, waiting for transfers between devices, local(): lax.psum_scatter(out_local.astype(jnp.bfloat16), 'fsdp', scatter_dimensio...  23.6 us
    all_gather x1, blocking collectives, local(): lax.all_gather(low_vec, 'fsdp', axis=1, tiled=True)  23.1 us
  transfers between devices with their start and end apart: 20, of which 17 were waited for; matrix products, arithmetic and copies ran while one was open for 12% of the time, Pallas kernels for 0%

profile of v1, /device:TPU:0, one launch (start us, length us, event | category | flops | bytes accessed | tf_op | source)
XLA Modules:
  0.0 584.8 jit_solution(15969269082935800062)
XLA Ops:
  11.0 23.1 %all-gather = bf16[16,48,4]{1,2,0:T(4,128)(2,1)S(1)} all-gather(bf16[1,48,4]{1,2,0:T(4,128)(2,1)S(1)} %convert_bitcast_fusion), channel_id=1, replica_groups=mesh['dp'=2,'fsdp'=16] {'fsdp'}, dimensions={0}, use_global_device_ids=true | all-gather | bytes 6528 | tf_op jit(solution)/shard_map/all_gather | solution.py:219
  35.3 38.1 %all-gather.6.cloned.1.call-done = bf16[3840,768]{1,0:T(8,128)(2,1)} async-done(((bf16[240,768]{1,0:T(8,128)(2,1)}), bf16[3840,768]{1,0:T(8,128)(2,1)}) %all-gather.6.cloned.1.call-update) | async-done | bytes 5898256 | tf_op jit(solution)/shard_map/all_gather | solution.py:212
  73.4 6.2 %convolution_convert_fusion.2 = bf16[512,3840]{1,0:T(8,128)(2,1)S(1)} fusion(bf16[512,768]{1,0:T(8,128)(2,1)S(1)} %copy-done.16, bf16[3840,768]{1,0:T(8,128)(2,1)} %all-gather.6.cloned.1.call-done), kind=kOutput, calls=%fused_computation.47 | convolution fusion | flops 3021864960 | bytes 10616832 | tf_op jit(solution)/shard_map/dot_general | solution.py:149
  82.7 66.3 %all-gather.4.cloned.1.call-done = bf16[768,5376]{1,0:T(8,128)(2,1)} async-done(((bf16[48,5376]{1,0:T(8,128)(2,1)}), bf16[768,5376]{1,0:T(8,128)(2,1)}) %all-gather.4.cloned.1.call-update) | async-done | bytes 8257552 | tf_op jit(solution)/shard_map/all_gather | solution.py:211
  149.0 7.2 %fusion.91 = f32[512,5376]{1,0:T(8,128)S(1)} fusion(bf16[768,5376]{1,0:T(8,128)(2,1)} %all-gather.4.cloned.1.call-done, bf16[512,768]{1,0:T(8,128)(2,1)S(1)} %copy-done.3, f32[768]{0:T(1024)S(1)} %get-tuple-element.90, f32[512]{0:T(512)S(1)} %fusion.81, f32[512]{0:T(512)S(1)} %broadcast_multiply_fusion.5), kind=kOutput, calls=%fused_computation.166 | convolution fusion | flops 4229824512 | bytes 20061184 | tf_op jit(solution)/shard_map/dot_general | solution.py:121
  156.2 6.6 %multiply_convert_fusion.1 = (bf16[512,3072]{1,0:T(8,128)(2,1)}, bf16[512,3072]{1,0:T(8,128)(2,1)}) fusion(f32[512,5376]{1,0:T(8,128)S(1)} %fusion.91, bf16[512,3840]{1,0:T(8,128)(2,1)S(1)} %copy-done.13), kind=kLoop, calls=%fused_computation.39 | loop fusion | flops 36175872 | bytes 15728640 | tf_op jit(solution)/shard_map/convert.9
  175.2 5.8 fusion.62
  181.0 3.6 fusion.59
  184.5 7.2 %multiply_reduce_fusion = (f32[12,512]{1,0:T(8,128)}, f32[12,512,512]{1,2,0:T(8,128)}) fusion(f32[12,512,512]{1,2,0:T(8,128)S(1)} %get-tuple-element.127, f32[12,512]{1,0:T(8,128)S(1)} %log_add_fusion, pred[512,512]{0,1:T(8,128)(4,1)S(1)} %broadcast_compare_fusion, bf16[512,12,64]{0,2,1:T(8,128)(2,1)S(1)} %bitcast.90, bf16[512,12,64]{0,2,1:T(8,128)(2,1)S(1)} %bitcast.92), kind=kOutput, calls=%fused_computation.3 | convolution fusion | flops 415229952 | bytes 27049984 | tf_op jit(solution)/shard_map/while/body/eval_jaxpr/qhd,khd->hqk/dot_general | solution.py:94
  196.3 10.0 %multiply_convert_fusion = bf16[12,512,512]{1,2,0:T(8,128)(2,1)S(1)} fusion(f32[12,512,512]{1,2,0:T(8,128)} %get-tuple-element.129, f32[12,512,512]{1,2,0:T(8,128)} %copy-done, f32[12,512]{1,0:T(8,128)} %get-tuple-element.128, f32[12,512]{1,0:T(8,128)} %copy-done.30, pred[512,512]{0,1:T(8,128)(4,1)S(1)} %broadcast_compare_fusion), kind=kLoop, calls=%fused_computation.2 | loop fusion | flops 15728640 | bytes 31768576 | tf_op jit(solution)/shard_map/while/body/eval_jaxpr/convert_element_type | solution.py:98
  227.2 9.0 %fusion.51 = (f32[512]{0:T(512)S(1)}, f32[512,768]{1,0:T(8,128)S(1)}) fusion(bf16[512,768]{1,0:T(8,128)(2,1)S(1)} %copy-done.4, f32[768]{0:T(1024)S(1)} %copy-done.35, f32[512]{0:T(512)S(1)} %copy-done.37, bf16[768,5376]{1,0:T(8,128)(2,1)} %all-gather.4.cloned.1.call-done, bf16[512,3072]{1,0:T(8,128)(2,1)} %get-tuple-element.119, ...), kind=kOutput, calls=%fused_computation.73 | convolution fusion | flops 4251844096 | bytes 16129024 | tf_op jit(solution)/shard_map/dot_general | solution.py:169
  239.0 7.8 %convolution_convert_fusion.1 = bf16[3840,768]{1,0:T(8,128)(2,1)} fusion(bf16[512,768]{1,0:T(8,128)(2,1)S(1)} %copy-done.17, bf16[512,3072]{1,0:T(8,128)(2,1)} %get-tuple-element.118, bf16[512,768]{1,0:T(8,128)(2,1)} %copy.99), kind=kOutput, calls=%fused_computation.19 | convolution fusion | flops 3030712320 | bytes 10616832 | tf_op jit(solution)/shard_map/dot_general | solution.py:146
  248.4 8.8 %convolution_convert_fusion = bf16[768,5376]{1,0:T(8,128)(2,1)} fusion(bf16[512,3072]{1,0:T(8,128)(2,1)} %get-tuple-element.119, bf16[512,768]{1,0:T(8,128)(2,1)S(1)} %copy-done.21, bf16[512,768]{1,0:T(8,128)(2,1)S(1)} %copy-done.22, bf16[512,768]{1,0:T(8,128)(2,1)S(1)} %copy-done.23, bf16[512,768]{1,0:T(8,128)(2,1)S(1)} %copy-done.4, ...), kind=kOutput, calls=%fused_computation.12 | convolution fusion | flops 4255973376 | bytes 14556160 | tf_op jit(solution)/shard_map/dot_general | solution.py:166
  258.1 4.2 collective-permute-start.8
  263.6 4.4 collective-permute-start.9
  269.3 4.4 collective-permute-start.10
  275.0 4.4 collective-permute-start.11
  280.7 4.4 collective-permute-start.12
  286.4 4.4 collective-permute-start.13
  292.1 4.4 collective-permute-start.14
  297.9 5.7 collective-permute-done.7
  305.7 7.4 %fusion.67 = f32[512,5376]{1,0:T(8,128)S(1)} fusion(bf16[768,5376]{1,0:T(8,128)(2,1)} %all-gather.4.cloned.1.call-done, bf16[512,768]{1,0:T(8,128)(2,1)S(1)} %copy-done.4, f32[768]{0:T(1024)S(1)} %get-tuple-element.105, f32[512]{0:T(512)S(1)} %copy-done.43, f32[512]{0:T(512)S(1)} %copy-done.37), kind=kOutput, calls=%fused_computation.108 | convolution fusion | flops 4229824512 | bytes 20061184 | tf_op jit(solution)/shard_map/dot_general | solution.py:121
  313.2 4.0 copy-done.6
  325.2 8.9 %fusion.99 = (f32[12,512]{1,0:T(8,128)}, f32[12,512,512]{1,2,0:T(8,128)}) fusion(pred[512,512]{0,1:T(8,128)(4,1)S(1)} %broadcast_compare_fusion, f32[512,12,64]{0,2,1:T(8,128)S(1)} %bitcast.88, f32[12,64]{1,0:T(8,128)} %mul.474, f32[512,12]{0,1:T(8,128)S(1)} %get-tuple-element.136, f32[512,12]{0,1:T(8,128)S(1)} %broadcast_multiply_fusion.2, ...), kind=kOutput, calls=%fused_computation.170 | convolution fusion | flops 415629824 | bytes 16119808 | tf_op jit(solution)/shard_map/while/body/eval_jaxpr/sub | solution.py:64
  334.1 6.0 %fusion.58 = bf16[12,64,512]{2,1,0:T(8,128)(2,1)S(1)} fusion(bf16[512,12,64]{0,2,1:T(8,128)(2,1)} %bitcast.95, f32[12,512,512]{1,2,0:T(8,128)} %get-tuple-element.125, f32[12,512]{1,0:T(8,128)} %get-tuple-element.124), kind=kOutput, calls=%fused_computation.98 | convolution fusion | flops 409337856 | bytes 14180352 | tf_op jit(solution)/shard_map/while/body/eval_jaxpr/hqk,khd->qhd/dot_general | solution.py:67
  340.7 3.9 fusion.25
  344.7 6.8 %fusion.52 = bf16[512,768]{1,0:T(8,128)(2,1)} fusion(bf16[512,768]{1,0:T(8,128)(2,1)S(1)} %copy-done.5, bf16[3840,768]{1,0:T(8,128)(2,1)} %all-gather.6.cloned.1.call-done, bf16[512,3072]{1,0:T(8,128)(2,1)S(1)} %fusion.25, bf16[512,768]{1,0:T(8,128)(2,1)S(1)} %copy.86, f32[768]{0:T(1024)S(1)} %copy-done.51), kind=kOutput, calls=%fused_computation.74 | convolution fusion | flops 3029336064 | bytes 11406336 | tf_op jit(solution)/shard_map/dot_general | solution.py:132
  352.4 23.6 %reduce-scatter.8.cloned.1.call-done = bf16[240,768]{1,0:T(8,128)(2,1)} async-done(((bf16[3840,768]{1,0:T(8,128)(2,1)}), bf16[240,768]{1,0:T(8,128)(2,1)}) %reduce-scatter.8.cloned.1.call-update) | async-done | bytes 368656 | tf_op jit(solution)/shard_map/reduce_scatter | solution.py:229
  376.0 107.5 %reduce-scatter.6.cloned.1.call-done = bf16[48,5376]{1,0:T(8,128)(2,1)} async-done(((bf16[768,5376]{1,0:T(8,128)(2,1)}), bf16[48,5376]{1,0:T(8,128)(2,1)}) %reduce-scatter.6.cloned.1.call-update) | async-done | bytes 516112 | tf_op jit(solution)/shard_map/reduce_scatter | solution.py:226
  483.5 46.3 %all-reduce.2 = (f32[48,5376]{1,0:T(8,128)S(1)}, f32[240,768]{1,0:T(8,128)}, f32[4,48]{1,0:T(4,128)S(1)}) all-reduce(bf16[48,5376]{1,0:T(8,128)(2,1)} %reduce-scatter.6.cloned.1.call-done, bf16[240,768]{1,0:T(8,128)(2,1)} %reduce-scatter.8.cloned.1.call-done, bf16[4,48]{1,0:T(4,128)(2,1)S(1)} %copy.106), channel_id=1, replica_groups=mesh['dp'=2,'fsdp'=16] {'dp'}, use_global_device_ids=true, to_apply=%region_22.23 | all-reduce | flops 442560 | bytes 2655360 | tf_op jit(solution)/shard_map/psum | solution.py:236
  538.1 31.6 %psum.31 = f32[]{:T(128)} all-reduce(f32[]{:T(128)S(6)} %add.195), channel_id=1, replica_groups=mesh['dp'=2,'fsdp'=16] {'fsdp'}, use_global_device_ids=true, to_apply=%region_34.35 | all-reduce | flops 1 | bytes 8 | tf_op jit(solution)/shard_map/psum | solution.py:180
  571.1 3.6 add_multiply_fusion.1
  (221 shorter events, 80.9 us)
Async XLA Ops:
  7.2 66.2 %all-gather.6.cloned.1.call-start = ((), (), s32[]{:S(2)}) async-start(), calls=%async_computation.4 | async-start | bytes 6266880 | tf_op jit(solution)/shard_map/all_gather | solution.py:212
  9.3 25.1 %copy-start.3 = (bf16[512,768]{1,0:T(8,128)(2,1)S(1)}, bf16[512,768]{1,0:T(8,128)(2,1)}, u32[]{:S(2)}) copy-start(bf16[512,768]{1,0:T(8,128)(2,1)} %param.12) | copy-start | bytes 2359300
  9.3 139.7 %all-gather.4.cloned.1.call-start = ((), (), s32[]{:S(2)}) async-start(), calls=%async_computation.3 | async-start | bytes 8773632 | tf_op jit(solution)/shard_map/all_gather | solution.py:211
  10.2 341.3 %reduce-scatter.10.cloned.1.call-start = ((), (), s32[]{:S(2)}) async-start(), calls=%async_computation.7 | async-start | bytes 208896
  34.3 114.7 %copy-start.34 = (f32[768]{0:T(1024)}, f32[768]{0:T(1024)S(1)}, u32[]{:S(2)}) copy-start(f32[768]{0:T(1024)S(1)} %get-tuple-element.90) | copy-start | bytes 9220
  34.4 45.2 %copy-start.31 = (f32[12,64]{1,0:T(8,128)}, f32[12,64]{1,0:T(8,128)S(1)}, u32[]{:S(2)}) copy-start(f32[12,64]{1,0:T(8,128)S(1)} %mul.493) | copy-start | bytes 9220
  34.6 114.4 %copy-start.36 = (f32[512]{0:T(512)}, f32[512]{0:T(512)S(1)}, u32[]{:S(2)}) copy-start(f32[512]{0:T(512)S(1)} %broadcast_multiply_fusion.5) | copy-start | bytes 6148
  35.0 44.6 %copy-start.38 = (f32[512]{0:T(512)}, f32[512]{0:T(512)S(1)}, u32[]{:S(2)}) copy-start(f32[512]{0:T(512)S(1)} %fusion.50) | copy-start | bytes 6148
  35.0 114.0 %copy-start.42 = (f32[512]{0:T(512)}, f32[512]{0:T(512)S(1)}, u32[]{:S(2)}) copy-start(f32[512]{0:T(512)S(1)} %fusion.81) | copy-start | bytes 6148
  238.5 137.5 %reduce-scatter.8.cloned.1.call-start = ((), (), s32[]{:S(2)}) async-start(), calls=%async_computation.6 | async-start | bytes 6266880 | tf_op jit(solution)/shard_map/reduce_scatter | solution.py:229
  246.8 236.7 %reduce-scatter.6.cloned.1.call-start = ((), (), s32[]{:S(2)}) async-start(), calls=%async_computation.5 | async-start | bytes 8773632 | tf_op jit(solution)/shard_map/reduce_scatter | solution.py:226
  257.9 5.7 collective-permute-start
  258.1 5.5 collective-permute-start.8
  263.6 5.7 collective-permute-start.1
  263.6 5.7 collective-permute-start.9
  269.3 5.7 collective-permute-start.2
  269.3 5.7 collective-permute-start.10
  275.0 5.7 collective-permute-start.3
  275.0 5.7 collective-permute-start.11
  280.7 5.7 collective-permute-start.4
  280.7 5.7 collective-permute-start.12
  286.4 5.7 collective-permute-start.5
  286.4 5.7 collective-permute-start.13
  292.0 5.7 collective-permute-start.6
  292.1 5.8 collective-permute-start.14
  297.7 5.8 collective-permute-start.7
  351.5 183.7 %copy-start.8 = (f32[512,768]{1,0:T(8,128)S(1)}, f32[512,768]{1,0:T(8,128)}, u32[]{:S(2)}) copy-start(f32[512,768]{1,0:T(8,128)} %copy-done.7) | copy-start | bytes 4718596
  351.5 183.7 %copy-start.44 = (f32[512]{0:T(512)S(1)}, f32[512]{0:T(512)}, u32[]{:S(2)}) copy-start(f32[512]{0:T(512)} %copy-done.42) | copy-start | bytes 6148
  529.8 40.7 %copy-start.49 = (f32[4,48]{1,0:T(4,128)}, f32[4,48]{1,0:T(4,128)S(1)}, u32[]{:S(2)}) copy-start(f32[4,48]{1,0:T(4,128)S(1)} %get-tuple-element.108) | copy-start | bytes 2308
  529.8 44.9 %copy-start.11 = (f32[48,5376]{1,0:T(8,128)}, f32[48,5376]{1,0:T(8,128)S(1)}, u32[]{:S(2)}) copy-start(f32[48,5376]{1,0:T(8,128)S(1)} %get-tuple-element.106) | copy-start | bytes 3096580
  535.2 35.3 %copy-start.52 = (f32[4,48]{1,0:T(4,128)S(1)}, f32[4,48]{1,0:T(4,128)}, u32[]{:S(2)}) copy-start(f32[4,48]{1,0:T(4,128)} %param.20) | copy-start | bytes 2308
  535.3 35.3 %copy-start.53 = (f32[4,48]{1,0:T(4,128)S(1)}, f32[4,48]{1,0:T(4,128)}, u32[]{:S(2)}) copy-start(f32[4,48]{1,0:T(4,128)} %param.23) | copy-start | bytes 2308
  (42 other events, 175.1 us)
Sparse Core Ops, SparseCore 0:
  10.9 62.4 all-gather.5
  76.3 72.6 all-gather.3
  238.7 51.8 reduce-scatter.9
  294.3 81.6 reduce-scatter.7
  380.5 102.9 reduce-scatter.5
